TPU v7x, 512 devices: a whole 4x8x8 slice. The times are simulated.
512 devices in a mesh: depth: 4 (over x), row: 8 (over z_hi, core), col: 16 (over z_lo, y).
Axes of the slice: x: 4, y: 8, z: 8 (z_hi: 4, z_lo: 2; z = z_hi * 2 + z_lo), core: 2. Of those that a mesh axis runs over, the one named last changes fastest.
Arguments:
- tokens: bfloat16 [512, 6144], P(('depth', 'row'), 'col'), may hold values from -6 to 6
- grad_out: bfloat16 [512, 6144], P(('depth', 'row'), 'col'), may hold values from -6 to 6
- w_up: bfloat16 [6144, 24576], P(('col', 'depth'), 'row'), may hold values from -0.078125 to 0.078125
- w_down: bfloat16 [6144, 24576], P(('col', 'depth'), 'row'), may hold values from -0.0390625 to 0.0390625
Outputs:
- grad_in: bfloat16 [512, 6144], P(('depth', 'row'), 'col')
- grad_up: bfloat16 [6144, 24576], P(('col', 'depth'), 'row')
- grad_down: bfloat16 [6144, 24576], P(('col', 'depth'), 'row')
All inputs are finite; a program needn't handle non-finite values.
Results may differ from a plain program's by a relative error of at most 0.03.
Values may be sent and summed in bfloat16 or wider, within the bound.
No kernel may reach another device: no remote copies, remote signals or barrier semaphores. Data moves between devices by JAX's collectives and lax.ppermute only.
A program may use at most 64 MiB of HBM per device.

v0:
```python
import math
import jax
import jax.numpy as jnp
from jax import lax
from jax.sharding import PartitionSpec as P


def gelu_parts(hidden):
    coeff = math.sqrt(2.0 / math.pi)
    cube = hidden * hidden * hidden
    slope_in = jnp.tanh(coeff * (hidden + 0.044715 * cube))
    value = 0.5 * hidden * (1.0 + slope_in)
    slope = 0.5 * (1.0 + slope_in) + 0.5 * hidden * (1.0 - slope_in * slope_in) * coeff * (
        1.0 + 3.0 * 0.044715 * hidden * hidden
    )
    return (value, slope)


def body(tokens, grad_out, w_up, w_down):
    depth_pos = lax.axis_index("depth")
    up_block, down_block = (
        lax.all_gather(w_up, "depth", axis=0, tiled=True),
        lax.all_gather(w_down, "depth", axis=0, tiled=True),
    )
    x_rows, dy_rows = (
        lax.all_gather(tokens, ("depth", "row"), axis=0, tiled=True),
        lax.all_gather(grad_out, ("depth", "row"), axis=0, tiled=True),
    )
    own_count = x_rows.shape[0] // lax.axis_size("depth")
    own_start = depth_pos * own_count
    x_own = lax.dynamic_slice_in_dim(x_rows, own_start, own_count, 0)
    dy_own = lax.dynamic_slice_in_dim(dy_rows, own_start, own_count, 0)
    narrow = w_up.shape[0]
    dy_narrow = lax.dynamic_slice_in_dim(dy_rows, depth_pos * narrow, narrow, 1)
    pre_part = jnp.dot(x_rows, up_block, preferred_element_type=jnp.float32)
    grad_part = jnp.dot(dy_own, down_block, preferred_element_type=jnp.float32)
    hidden_pre, act_grad = (
        lax.psum(pre_part.astype(jnp.bfloat16), "col").astype(jnp.float32),
        lax.psum(grad_part.astype(jnp.bfloat16), "col").astype(jnp.float32),
    )
    act_value, slope = gelu_parts(hidden_pre)
    act_rows = act_value.astype(jnp.bfloat16)
    slope_own = lax.dynamic_slice_in_dim(slope, own_start, own_count, 0)
    hidden_grad = (act_grad * slope_own).astype(jnp.bfloat16)
    grad_up = lax.psum_scatter(
        lax.dot_general(
            x_own, hidden_grad, (((0,), (0,)), ((), ())), preferred_element_type=jnp.float32
        ).astype(jnp.bfloat16),
        "depth",
        scatter_dimension=0,
        tiled=True,
    )
    grad_in = lax.psum_scatter(
        lax.dot_general(
            hidden_grad, up_block, (((1,), (1,)), ((), ())), preferred_element_type=jnp.float32
        ).astype(jnp.bfloat16),
        "row",
        scatter_dimension=0,
        tiled=True,
    )
    grad_down = lax.dot_general(
        dy_narrow, act_rows, (((0,), (0,)), ((), ())), preferred_element_type=jnp.float32
    ).astype(jnp.bfloat16)
    return (grad_in, grad_up, grad_down)


def solution(mesh):
    placed = (
        P(("depth", "row"), "col"),
        P(("depth", "row"), "col"),
        P(("col", "depth"), "row"),
        P(("col", "depth"), "row"),
    )
    return jax.shard_map(
        body,
        mesh=mesh,
        in_specs=placed,
        out_specs=(
            P(("depth", "row"), "col"),
            P(("col", "depth"), "row"),
            P(("col", "depth"), "row"),
        ),
        check_vma=False,
    )
```

profile of v0, /device:TPU:1, one launch (start us, length us, event | category | flops | bytes accessed | tf_op | source)
XLA Modules:
  0.0 356.0 jit_solution(12280223903495737786)
XLA Ops:
  7.2 0.0 all-gather.5.cloned.1.call-start
  7.2 0.7 all-gather.5.cloned.1.call-update
  7.9 0.0 all-gather.3.cloned.1.call-start
  7.9 0.7 all-gather.3.cloned.1.call-update
  8.6 0.0 all-reduce.3.cloned.1.call-start
  8.7 53.1 %all_gather.14 = bf16[512,384]{1,0:T(8,128)(2,1)S(1)} all-gather(bf16[16,384]{1,0:T(8,128)(2,1)} %param.4), channel_id=1, replica_groups=mesh['depth'=4,'row'=8,'col'=16] {'depth','row'}, dimensions={0}, use_global_device_ids=true | all-gather | bytes 405504 | tf_op jit(solution)/shard_map/all_gather | solution.py:26
  61.8 0.0 copy-start.4
  61.8 40.9 %all_gather.12 = bf16[512,384]{1,0:T(8,128)(2,1)S(1)} all-gather(bf16[16,384]{1,0:T(8,128)(2,1)} %param.5), channel_id=1, replica_groups=mesh['depth'=4,'row'=8,'col'=16] {'depth','row'}, dimensions={0}, use_global_device_ids=true | all-gather | bytes 405504 | tf_op jit(solution)/shard_map/all_gather | solution.py:27
  102.7 0.0 all-gather.5.cloned.1.call-done
  102.7 5.1 %convolution_convert_fusion = bf16[512,3072]{1,0:T(8,128)(2,1)} fusion(bf16[512,384]{1,0:T(8,128)(2,1)S(1)} %all_gather.14, bf16[384,3072]{1,0:T(8,128)(2,1)} %all-gather.5.cloned.1.call-done), kind=kOutput, calls=%fused_computation.6 | convolution fusion | flops 1209532416 | bytes 5898240 | tf_op jit(solution)/shard_map/dot_general | solution.py:35
  107.8 0.0 copy-done.4
  107.8 0.0 all-gather.3.cloned.1.call-done
  107.8 3.2 convolution_convert_fusion.2
  111.0 0.0 all-reduce.3.cloned.1.call-update
  111.0 0.0 reduce-scatter.3.cloned.1.call-start
  111.1 145.0 %all-reduce.3.cloned.1.call-done = (bf16[512,3072]{1,0:T(8,128)(2,1)}, bf16[128,3072]{1,0:T(8,128)(2,1)}) async-done(((bf16[512,3072]{1,0:T(8,128)(2,1)}, bf16[128,3072]{1,0:T(8,128)(2,1)}), (bf16[512,3072]{1,0:T(8,128)(2,1)}, bf16[128,3072]{1,0:T(8,128)(2,1)})) %all-reduce.3.cloned.1.call-update) | async-done | bytes 3932176 | tf_op jit(solution)/shard_map/psum | solution.py:38
  256.1 0.0 copy-start
  256.1 2.8 convert_element_type.30
  258.9 0.0 copy-done
  258.9 0.0 copy-start.3
  258.9 2.6 fusion.3
  261.5 0.0 copy-done.3
  261.5 0.0 copy-start.2
  261.5 0.7 fusion.8
  262.2 0.0 copy-start.1
  262.3 0.9 copy-done.1
  263.1 0.0 copy-done.2
  263.2 1.5 convolution_convert_fusion.4
  264.6 0.0 reduce-scatter.3.cloned.1.call-update
  264.7 0.0 reduce-scatter.5.cloned.1.call-start
  264.7 3.4 convolution_convert_fusion.1
  268.1 0.0 reduce-scatter.5.cloned.1.call-update
  268.2 3.3 convolution_convert_fusion.3
  271.5 38.2 %reduce-scatter.3.cloned.1.call-done = bf16[16,384]{1,0:T(8,128)(2,1)} async-done(((bf16[128,384]{1,0:T(8,128)(2,1)}), bf16[16,384]{1,0:T(8,128)(2,1)}) %reduce-scatter.3.cloned.1.call-update) | async-done | bytes 12304 | tf_op jit(solution)/shard_map/reduce_scatter | solution.py:53
  309.7 39.8 %reduce-scatter.5.cloned.1.call-done = bf16[96,3072]{1,0:T(8,128)(2,1)} async-done(((bf16[384,3072]{1,0:T(8,128)(2,1)}), bf16[96,3072]{1,0:T(8,128)(2,1)}) %reduce-scatter.5.cloned.1.call-update) | async-done | bytes 589840 | tf_op jit(solution)/shard_map/reduce_scatter | solution.py:45
Async XLA Ops:
  7.2 95.5 %all-gather.5.cloned.1.call-start = ((), (), s32[]{:S(2)}) async-start(), calls=%async_computation.3 | async-start | bytes 2949120 | tf_op jit(solution)/shard_map/all_gather | solution.py:22
  7.9 99.9 %all-gather.3.cloned.1.call-start = ((), (), s32[]{:S(2)}) async-start(), calls=%async_computation.2 | async-start | bytes 2949120 | tf_op jit(solution)/shard_map/all_gather | solution.py:23
  8.6 247.4 %all-reduce.3.cloned.1.call-start = ((), (), s32[]{:S(2)}) async-start(), calls=%async_computation.6 | async-start | bytes 7864320 | tf_op jit(solution)/shard_map/psum | solution.py:38
  61.8 46.0 %copy-start.4 = (bf16[512,384]{1,0:T(8,128)(2,1)}, bf16[512,384]{1,0:T(8,128)(2,1)S(1)}, u32[]{:S(2)}) copy-start(bf16[512,384]{1,0:T(8,128)(2,1)S(1)} %all_gather.14) | copy-start | bytes 1179652
  111.0 198.7 %reduce-scatter.3.cloned.1.call-start = ((), (), s32[]{:S(2)}) async-start(), calls=%async_computation.4 | async-start | bytes 110592 | tf_op jit(solution)/shard_map/reduce_scatter | solution.py:53
  256.1 2.9 copy-start
  258.9 2.6 copy-start.3
  261.5 1.7 copy-start.2
  262.2 0.9 copy-start.1
  264.7 84.8 %reduce-scatter.5.cloned.1.call-start = ((), (), s32[]{:S(2)}) async-start(), calls=%async_computation.5 | async-start | bytes 2949120 | tf_op jit(solution)/shard_map/reduce_scatter | solution.py:45
Sparse Core Ops, SparseCore 0:
  10.1 44.9 all-gather.4
  57.2 38.4 all-gather.2
  111.1 144.8 all-reduce.2
  264.8 44.8 reduce-scatter.2
  312.9 36.4 reduce-scatter.4
where the time goes:
time: 356 us
  waiting for transfers between devices  224 us (63%)
  blocking collectives  94 us (26%)
  matrix products  16.5 us (5%)
  between operations  13.9 us (4%)
  other arithmetic  6.11 us (2%)
    psum x1, waiting for transfers between devices, body(): lax.psum(pre_part.astype(jnp.bfloat16), 'col').astype(jnp.float32)  145 us
    all_gather x1, blocking collectives, body(): lax.all_gather(tokens, ('depth', 'row'), axis=0, tiled=True)  53.1 us
    all_gather x1, blocking collectives, body(): lax.all_gather(grad_out, ('depth', 'row'), axis=0, tiled=True)  40.9 us
    reduce_scatter x1, waiting for transfers between devices, body(): lax.psum_scatter(lax.dot_general(x_own, hidden_grad, (((0,), (0,)), ((),...  39.8 us
    reduce_scatter x1, waiting for transfers between devices, body(): lax.psum_scatter(lax.dot_general(hidden_grad, up_block, (((1,), (1,)), ((...  38.2 us
  transfers between devices with their start and end apart: 5, of which 3 were waited for; matrix products, arithmetic and copies ran while one was open for 3% of the time, Pallas kernels for 0%

commit v1 on v0

--- a/solution.py
+++ b/solution.py
@@ -22,8 +22,17 @@
         lax.all_gather(w_up, "depth", axis=0, tiled=True),
         lax.all_gather(w_down, "depth", axis=0, tiled=True),
     )
+
+    def clusters_wait(slab_in):
+        return jnp.concatenate(
+            lax.all_to_all(
+                jnp.stack([slab_in] * lax.axis_size(("depth", "row")), 0), ("depth", "row"), 0, 0
+            ),
+            axis=0,
+        )
+
     x_rows, dy_rows = (
-        lax.all_gather(tokens, ("depth", "row"), axis=0, tiled=True),
+        clusters_wait(tokens),
         lax.all_gather(grad_out, ("depth", "row"), axis=0, tiled=True),
     )
     own_count = x_rows.shape[0] // lax.axis_size("depth")

time: 356 us -> 349 us (0.980)
  blocking collectives: 94 us -> 50.2 us
  waiting for transfers between devices: 224 us -> 243 us
  starting transfers between devices: 0.2 us -> 14.6 us
    all_gather x1 -> x0, blocking collectives: 53.1 us -> none  [body(): lax.all_gather(tokens, ('depth', 'row'), axis=0, tiled=True)]
    all_gather x1, waiting for transfers between devices: 0.01 us -> 15.6 us  [body(): lax.all_gather(w_down, 'depth', axis=0, tiled=True)]
    all_to_all x0 -> x1, starting transfers between devices: none -> 14.4 us  [clusters_wait(): lax.all_to_all(jnp.stack([slab_in] * lax.axis_size(('depth', 'row')), 0),...]
    all_gather x1, blocking collectives: 40.9 us -> 50.2 us  [body(): lax.all_gather(grad_out, ('depth', 'row'), axis=0, tiled=True)]
    psum x1, waiting for transfers between devices: 145 us -> 149 us  [body(): lax.psum(pre_part.astype(jnp.bfloat16), 'col').astype(jnp.float32)]
  transfers between devices with their start and end apart: 5 -> 6, of which waited for: 3 -> 4; matrix products, arithmetic and copies ran while one was open for 3% -> 4% of each run, Pallas kernels for 0% -> 0%
where the time goes in v1:
time: 349 us; the launch traced here: 348 us
  waiting for transfers between devices  243 us (70%)
  blocking collectives  50.2 us (14%)
  matrix products  17.6 us (5%)
  starting transfers between devices  14.6 us (4%)
  between operations  13.9 us (4%)
  other arithmetic  6.11 us (2%)
    psum x1, waiting for transfers between devices, body(): lax.psum(pre_part.astype(jnp.bfloat16), 'col').astype(jnp.float32)  149 us
    all_gather x1, blocking collectives, body(): lax.all_gather(grad_out, ('depth', 'row'), axis=0, tiled=True)  50.2 us
    reduce_scatter x1, waiting for transfers between devices, body(): lax.psum_scatter(lax.dot_general(x_own, hidden_grad, (((0,), (0,)), ((),...  39.8 us
    reduce_scatter x1, waiting for transfers between devices, body(): lax.psum_scatter(lax.dot_general(hidden_grad, up_block, (((1,), (1,)), ((...  37.3 us
    all_gather x1, waiting for transfers between devices, body(): lax.all_gather(w_down, 'depth', axis=0, tiled=True)  15.6 us
    all_to_all x1, starting transfers between devices, clusters_wait(): lax.all_to_all(jnp.stack([slab_in] * lax.axis_size(('depth', 'row')), 0),...  14.4 us
  transfers between devices with their start and end apart: 6, of which 4 were waited for; matrix products, arithmetic and copies ran while one was open for 4% of the time, Pallas kernels for 0%

profile of v1, /device:TPU:1, one launch (start us, length us, event | category | flops | bytes accessed | tf_op | source)
XLA Modules:
  0.0 348.1 jit_solution(7975840372301254546)
XLA Ops:
  7.2 0.0 all-gather.5.cloned.1.call-start
  7.2 0.7 all-gather.5.cloned.1.call-update
  7.9 0.0 all-gather.3.cloned.1.call-start
  7.9 0.7 all-gather.3.cloned.1.call-update
  8.6 1.5 stack.2
  10.1 14.4 %all-to-all-start = ((bf16[32,16,384]{2,1,0:T(8,128)(2,1)}), bf16[32,16,384]{2,1,0:T(8,128)(2,1)S(1)}, u32[]{:S(2)}, u32[]{:S(2)}) async-start(bf16[32,16,384]{2,1,0:T(8,128)(2,1)} %stack.2), calls=%async_computation | async-start | bytes 786432 | tf_op jit(solution)/shard_map/all_to_all | solution.py:28
  24.6 0.0 all-reduce.3.cloned.1.call-start
  24.6 50.2 %all_gather.9 = bf16[512,384]{1,0:T(8,128)(2,1)S(1)} all-gather(bf16[16,384]{1,0:T(8,128)(2,1)} %param.5), channel_id=1, replica_groups=mesh['depth'=4,'row'=8,'col'=16] {'depth','row'}, dimensions={0}, use_global_device_ids=true | all-gather | bytes 405504 | tf_op jit(solution)/shard_map/all_gather | solution.py:36
  74.8 0.0 copy-start.4
  74.8 0.0 all-to-all-done
  74.8 0.0 all-gather.5.cloned.1.call-done
  74.8 5.3 %convolution_convert_fusion = bf16[512,3072]{1,0:T(8,128)(2,1)} fusion(bf16[512,384]{1,0:T(8,128)(2,1)S(1)} %bitcast.7, bf16[384,3072]{1,0:T(8,128)(2,1)} %all-gather.5.cloned.1.call-done), kind=kOutput, calls=%fused_computation.6 | convolution fusion | flops 1209532416 | bytes 5898240 | tf_op jit(solution)/shard_map/dot_general | solution.py:44
  80.1 15.6 %all-gather.3.cloned.1.call-done = bf16[384,3072]{1,0:T(8,128)(2,1)} async-done(((bf16[96,3072]{1,0:T(8,128)(2,1)}), bf16[384,3072]{1,0:T(8,128)(2,1)}) %all-gather.3.cloned.1.call-update) | async-done | bytes 2359312 | tf_op jit(solution)/shard_map/all_gather | solution.py:23
  95.6 3.2 convolution_convert_fusion.2
  98.8 0.0 copy-done.4
  98.8 0.0 all-reduce.3.cloned.1.call-update
  98.9 0.0 reduce-scatter.3.cloned.1.call-start
  98.9 149.2 %all-reduce.3.cloned.1.call-done = (bf16[512,3072]{1,0:T(8,128)(2,1)}, bf16[128,3072]{1,0:T(8,128)(2,1)}) async-done(((bf16[512,3072]{1,0:T(8,128)(2,1)}, bf16[128,3072]{1,0:T(8,128)(2,1)}), (bf16[512,3072]{1,0:T(8,128)(2,1)}, bf16[128,3072]{1,0:T(8,128)(2,1)})) %all-reduce.3.cloned.1.call-update) | async-done | bytes 3932176 | tf_op jit(solution)/shard_map/psum | solution.py:47
  248.2 0.0 copy-start
  248.2 2.8 convert_element_type.30
  251.0 0.0 copy-done
  251.0 0.0 copy-start.3
  251.0 2.6 fusion.3
  253.6 0.0 copy-done.3
  253.6 0.0 copy-start.2
  253.6 0.7 fusion.8
  254.3 0.0 copy-start.1
  254.3 0.9 copy-done.1
  255.2 0.0 copy-done.2
  255.3 1.5 convolution_convert_fusion.4
  256.7 0.0 reduce-scatter.3.cloned.1.call-update
  256.8 0.0 reduce-scatter.5.cloned.1.call-start
  256.8 3.4 convolution_convert_fusion.1
  260.2 0.0 reduce-scatter.5.cloned.1.call-update
  260.2 4.2 %convolution_convert_fusion.3 = bf16[96,3072]{1,0:T(8,128)(2,1)} fusion(bf16[512,3072]{1,0:T(8,128)(2,1)S(1)} %copy-done, bf16[512,384]{1,0:T(8,128)(2,1)} %copy-done.4, s32[]{:T(128)S(6)} %select_n.9), kind=kOutput, calls=%fused_computation.9 | convolution fusion | flops 318013440 | bytes 3866628 | tf_op jit(solution)/shard_map/dot_general | solution.py:70
  264.5 37.3 %reduce-scatter.3.cloned.1.call-done = bf16[16,384]{1,0:T(8,128)(2,1)} async-done(((bf16[128,384]{1,0:T(8,128)(2,1)}), bf16[16,384]{1,0:T(8,128)(2,1)}) %reduce-scatter.3.cloned.1.call-update) | async-done | bytes 12304 | tf_op jit(solution)/shard_map/reduce_scatter | solution.py:62
  301.8 39.8 %reduce-scatter.5.cloned.1.call-done = bf16[96,3072]{1,0:T(8,128)(2,1)} async-done(((bf16[384,3072]{1,0:T(8,128)(2,1)}), bf16[96,3072]{1,0:T(8,128)(2,1)}) %reduce-scatter.5.cloned.1.call-update) | async-done | bytes 589840 | tf_op jit(solution)/shard_map/reduce_scatter | solution.py:54
Async XLA Ops:
  7.2 67.6 %all-gather.5.cloned.1.call-start = ((), (), s32[]{:S(2)}) async-start(), calls=%async_computation.4 | async-start | bytes 2949120 | tf_op jit(solution)/shard_map/all_gather | solution.py:22
  7.9 87.7 %all-gather.3.cloned.1.call-start = ((), (), s32[]{:S(2)}) async-start(), calls=%async_computation.3 | async-start | bytes 2949120 | tf_op jit(solution)/shard_map/all_gather | solution.py:23
  10.1 64.7 %all-to-all-start = ((bf16[32,16,384]{2,1,0:T(8,128)(2,1)}), bf16[32,16,384]{2,1,0:T(8,128)(2,1)S(1)}, u32[]{:S(2)}, u32[]{:S(2)}) async-start(bf16[32,16,384]{2,1,0:T(8,128)(2,1)} %stack.2), calls=%async_computation | async-start | bytes 786432 | tf_op jit(solution)/shard_map/all_to_all | solution.py:28
  24.6 223.6 %all-reduce.3.cloned.1.call-start = ((), (), s32[]{:S(2)}) async-start(), calls=%async_computation.7 | async-start | bytes 7864320 | tf_op jit(solution)/shard_map/psum | solution.py:47
  74.8 24.1 %copy-start.4 = (bf16[512,384]{1,0:T(8,128)(2,1)}, bf16[512,384]{1,0:T(8,128)(2,1)S(1)}, u32[]{:S(2)}) copy-start(bf16[512,384]{1,0:T(8,128)(2,1)S(1)} %all_gather.9) | copy-start | bytes 1179652
  98.9 202.9 %reduce-scatter.3.cloned.1.call-start = ((), (), s32[]{:S(2)}) async-start(), calls=%async_computation.5 | async-start | bytes 110592 | tf_op jit(solution)/shard_map/reduce_scatter | solution.py:62
  248.2 2.9 copy-start
  251.0 2.6 copy-start.3
  253.6 1.7 copy-start.2
  254.3 0.9 copy-start.1
  256.8 84.8 %reduce-scatter.5.cloned.1.call-start = ((), (), s32[]{:S(2)}) async-start(), calls=%async_computation.6 | async-start | bytes 2949120 | tf_op jit(solution)/shard_map/reduce_scatter | solution.py:54
Sparse Core Ops, SparseCore 0:
  10.1 46.4 all-gather.4
  58.7 36.9 all-gather.2
  99.0 149.1 all-reduce.2
  256.9 44.8 reduce-scatter.2
  305.1 36.4 reduce-scatter.4
